TPU v7x, 32 devices: a whole 2x2x4 slice. The times are simulated.
32 devices in a mesh: dp: 8 (over y, x, core), fsdp: 4 (over z).
Axes of the slice: x: 2, y: 2, z: 4, core: 2. Of those that a mesh axis runs over, the one named last changes fastest.
Arguments:
- teacher_in: bfloat16 [8, 512, 4096], P('dp', 'fsdp'), may hold values from -6 to 6
- teacher_out: bfloat16 [8, 512, 4096], P('dp', 'fsdp'), may hold values from -6 to 6
- owner_section: int32 [4], P('fsdp'), may hold values from 0 to 7
- gate_blocks: bfloat16 [32, 10, 128, 128], P('dp', None, 'fsdp'), may hold values from -0.15625 to 0.15625
- up_blocks: bfloat16 [32, 10, 128, 128], P('dp', None, 'fsdp'), may hold values from -0.15625 to 0.15625
- down_blocks: bfloat16 [32, 10, 128, 128], P('dp', None, 'fsdp'), may hold values from -0.15625 to 0.15625
- input_lists: int32 [32, 10], P('dp'), may hold values from 0 to 31, as said below
- input_counts: int32 [32], P('dp'), may hold values from 6 to 10, as said below
- output_lists: int32 [32, 10], P('dp'), may hold values from 0 to 31, as said below
- output_counts: int32 [32], P('dp'), may hold values from 6 to 10, as said below
Outputs:
- grad_gate: bfloat16 [32, 10, 128, 128], P('dp', None, 'fsdp')
- grad_up: bfloat16 [32, 10, 128, 128], P('dp', None, 'fsdp')
- grad_down: bfloat16 [32, 10, 128, 128], P('dp', None, 'fsdp')
Inputs may be any that keep to these rules, and one draw needn't show every extreme that they name: `input_lists`: the first 10 entries of each row are distinct; entries at dead slots are ignored. `input_counts`: among the hidden blocks of one index of dp, one block has exactly 10 live slots. `output_lists`: the first 10 entries of each row are distinct; entries at dead slots are ignored. `output_counts`: among the hidden blocks of one index of dp, one block has exactly 10 live slots.
All inputs are finite; a program needn't handle non-finite values.
Results may differ from a plain program's by a relative error of at most 0.025.
Values may be sent and summed in bfloat16 or wider, within the bound.
No kernel may reach another device: no remote copies, remote signals or barrier semaphores. Data moves between devices by JAX's collectives and lax.ppermute only.
A program may use at most 64 MiB of HBM per device.

v0:
```python
import jax
import jax.numpy as jnp
from jax import lax
from jax.sharding import PartitionSpec as P


def broadcast(shard, axis, root):
    mine = lax.axis_index(axis) == root
    return lax.psum(jnp.where(mine, shard, jnp.zeros_like(shard)), axis)


def live_mask(counts, slot_count):
    positions = jnp.arange(slot_count, dtype=jnp.int32)
    return (positions[None, :] < counts[:, None])[:, :, None, None]


def shards(
    teacher_in,
    teacher_out,
    owner_section,
    gate_blocks,
    up_blocks,
    down_blocks,
    input_lists,
    input_counts,
    output_lists,
    output_counts,
):
    root_section = owner_section[0]
    local_in = teacher_in[0]
    local_out = teacher_out[0]
    micro_count = lax.axis_size("fsdp")
    rows_in = broadcast(local_in, "dp", root_section)
    gate_full, up_full, down_full = (
        lax.all_gather(gate_blocks, "fsdp", axis=2, tiled=True),
        lax.all_gather(up_blocks, "fsdp", axis=2, tiled=True),
        lax.all_gather(down_blocks, "fsdp", axis=2, tiled=True),
    )
    slot_count = input_lists.shape[1]
    block_edge = gate_full.shape[3]
    tok_rows = rows_in.shape[0]
    model_width = rows_in.shape[1]
    row_blocks = model_width // block_edge
    input_live = live_mask(input_counts, slot_count)
    output_live = live_mask(output_counts, slot_count)
    zero_value = jnp.zeros((), jnp.bfloat16)
    gate_live = jnp.where(input_live, gate_full, zero_value)
    up_live = jnp.where(input_live, up_full, zero_value)
    down_live = jnp.where(output_live, down_full, zero_value)
    picked = rows_in.reshape(tok_rows, row_blocks, block_edge)[:, input_lists]
    gate_pre = jnp.einsum("tfki,fkio->tfo", picked, gate_live, preferred_element_type=jnp.float32)
    up_pre = jnp.einsum("tfki,fkio->tfo", picked, up_live, preferred_element_type=jnp.float32)
    sigmoid_gate = jax.nn.sigmoid(gate_pre)
    activated = gate_pre * sigmoid_gate
    hidden = (activated * up_pre).astype(jnp.bfloat16)
    pieces = jnp.einsum("tfi,fkio->tfko", hidden, down_live, preferred_element_type=jnp.float32)
    blank_out = jnp.zeros((tok_rows, row_blocks, block_edge), jnp.float32)
    partial_out = blank_out.at[:, output_lists].add(pieces).reshape(tok_rows, model_width)
    is_owner = lax.axis_index("dp") == root_section
    own_term = jnp.where(is_owner, local_out.astype(jnp.float32), jnp.float32(0.0))
    residual_rows = lax.psum((partial_out - own_term).astype(jnp.bfloat16), "dp").astype(
        jnp.float32
    )
    scaled_error = (residual_rows / micro_count).astype(jnp.bfloat16)
    error_picked = scaled_error.reshape(tok_rows, row_blocks, block_edge)[:, output_lists]
    output_scale = output_live.astype(jnp.float32)
    input_scale = input_live.astype(jnp.float32)
    down_grad = (
        jnp.einsum("tfi,tfko->fkio", hidden, error_picked, preferred_element_type=jnp.float32)
        * output_scale
    )
    hidden_grad = jnp.einsum(
        "tfko,fkio->tfi", error_picked, down_live, preferred_element_type=jnp.float32
    )
    gate_error = (
        hidden_grad * up_pre * sigmoid_gate * (1.0 + gate_pre * (1.0 - sigmoid_gate))
    ).astype(jnp.bfloat16)
    up_error = (hidden_grad * activated).astype(jnp.bfloat16)
    gate_grad = (
        jnp.einsum("tfki,tfo->fkio", picked, gate_error, preferred_element_type=jnp.float32)
        * input_scale
    )
    up_grad = (
        jnp.einsum("tfki,tfo->fkio", picked, up_error, preferred_element_type=jnp.float32)
        * input_scale
    )
    gate_sum, up_sum, down_sum = (
        lax.psum_scatter(
            gate_grad.astype(jnp.bfloat16), "fsdp", scatter_dimension=2, tiled=True
        ).astype(jnp.float32),
        lax.psum_scatter(
            up_grad.astype(jnp.bfloat16), "fsdp", scatter_dimension=2, tiled=True
        ).astype(jnp.float32),
        lax.psum_scatter(
            down_grad.astype(jnp.bfloat16), "fsdp", scatter_dimension=2, tiled=True
        ).astype(jnp.float32),
    )
    return (
        gate_sum.astype(jnp.bfloat16),
        up_sum.astype(jnp.bfloat16),
        down_sum.astype(jnp.bfloat16),
    )


def solution(mesh):
    return jax.shard_map(
        shards,
        mesh=mesh,
        in_specs=(
            P("dp", "fsdp", None),
            P("dp", "fsdp", None),
            P("fsdp"),
            P("dp", None, "fsdp", None),
            P("dp", None, "fsdp", None),
            P("dp", None, "fsdp", None),
            P("dp", None),
            P("dp"),
            P("dp", None),
            P("dp"),
        ),
        out_specs=(
            P("dp", None, "fsdp", None),
            P("dp", None, "fsdp", None),
            P("dp", None, "fsdp", None),
        ),
        check_vma=False,
    )
```

profile of v0, /device:TPU:0, one launch (start us, length us, event | category | flops | bytes accessed | tf_op | source)
XLA Modules:
  0.0 329.0 jit_solution(10549377895469457317)
XLA Ops:
  8.0 0.0 all-reduce.5.cloned.1.call-start
  8.7 1.6 copy.63
  10.3 0.1 broadcast_select_fusion.3
  10.4 1.3 copy.64
  11.7 0.0 all-reduce.5.cloned.1.call-update
  11.8 0.0 all-gather.6.cloned.1.call-start
  11.8 0.5 all-gather.6.cloned.1.call-update
  12.3 0.0 copy-start.9
  12.3 0.0 copy-start.10
  12.4 0.0 all-gather.8.cloned.1.call-start
  12.4 0.5 all-gather.8.cloned.1.call-update
  13.0 0.0 all-gather.4.cloned.1.call-start
  13.0 0.5 all-gather.4.cloned.1.call-update
  13.5 0.0 all-reduce.7.cloned.1.call-start
  13.6 0.0 copy-done.7
  13.6 0.1 reshape.108
  13.7 0.0 copy-done.8
  13.7 0.1 reshape.124
  13.8 0.0 copy-done.4
  13.8 1.3 copy.74
  15.1 0.0 copy-done.9
  15.1 0.1 iota_compare_fusion
  15.2 0.1 fusion.34
  15.3 56.3 %all-reduce.5.cloned.1.call-done = bf16[128,32,128]{2,0,1:T(8,128)(2,1)} async-done(((bf16[128,32,128]{2,0,1:T(8,128)(2,1)}), bf16[128,32,128]{2,0,1:T(8,128)(2,1)}) %all-reduce.5.cloned.1.call-update) | async-done | bytes 1048592 | tf_op jit(solution)/shard_map/psum | solution.py:9
  71.6 2.0 gather_fusion
  73.6 0.0 all-gather.6.cloned.1.call-done
  73.6 2.4 fusion.11
  76.1 5.8 %all-gather.8.cloned.1.call-done = bf16[4,10,128,128]{3,2,1,0:T(8,128)(2,1)} async-done(((bf16[4,10,32,128]{3,2,1,0:T(8,128)(2,1)}), bf16[4,10,128,128]{3,2,1,0:T(8,128)(2,1)}) %all-gather.8.cloned.1.call-update) | async-done | bytes 1310736 | tf_op jit(solution)/shard_map/all_gather | solution.py:36
  81.9 2.0 fusion.14
  83.9 0.0 copy-start.5
  83.9 0.1 fusion.23
  84.0 30.9 %all-gather.4.cloned.1.call-done = bf16[4,10,128,128]{3,2,1,0:T(8,128)(2,1)} async-done(((bf16[4,10,32,128]{3,2,1,0:T(8,128)(2,1)}), bf16[4,10,128,128]{3,2,1,0:T(8,128)(2,1)}) %all-gather.4.cloned.1.call-update) | async-done | bytes 1310736 | tf_op jit(solution)/shard_map/all_gather | solution.py:37
  114.9 2.0 fusion.17
  116.9 2.1 copy.72
  119.0 0.2 broadcast_in_dim.49
  119.2 6.5 %scatter_fusion = f32[128,32,128]{2,0,1:T(8,128)S(1)} fusion(f32[128,32,128]{2,0,1:T(8,128)S(1)} %broadcast_in_dim.49, s32[40]{0:T(128)S(1)} %reshape.124, f32[40,128,128]{2,1,0:T(8,128)} %copy.72), kind=kCustom, calls=%fused_computation.2 | custom fusion | flops 655360 | bytes 7864480 | tf_op jit(solution)/shard_map/scatter-add | solution.py:58
  125.8 1.8 copy.73
  127.6 2.9 fusion
  130.5 0.0 all-reduce.7.cloned.1.call-update
  130.5 0.0 all-reduce.9.cloned.1.call-start
  130.6 56.0 %all-reduce.7.cloned.1.call-done = bf16[128,4096]{0,1:T(8,128)(2,1)} async-done(((bf16[128,4096]{0,1:T(8,128)(2,1)}), bf16[128,4096]{0,1:T(8,128)(2,1)}) %all-reduce.7.cloned.1.call-update) | async-done | bytes 1048592 | tf_op jit(solution)/shard_map/psum | solution.py:61
  186.5 1.4 multiply_convert_fusion.3
  188.0 0.7 copy.75
  188.6 0.8 gather_fusion.1
  189.4 0.8 copy.76
  190.2 1.6 fusion.1
  191.8 3.7 %copy.81 = bf16[4,10,128,128]{3,0,1,2:T(4,128)(2,1)} copy(bf16[4,10,128,128]{2,3,1,0:T(8,128)(2,1)} %fusion.1) | data formatting | bytes 2621440 | tf_op jit(solution)/shard_map/convert_element_type | solution.py:95
  195.5 0.0 all-reduce.9.cloned.1.call-update
  195.6 0.0 reduce-scatter.3.cloned.1.call-start
  195.6 1.2 copy-done.1
  196.8 1.4 copy.65
  198.3 2.0 convolution_bitcast_fusion
  200.3 1.6 multiply_convert_fusion.2
  201.9 0.0 reduce-scatter.3.cloned.1.call-update
  202.0 0.0 reduce-scatter.5.cloned.1.call-start
  202.0 1.6 multiply_convert_fusion.1
  203.6 0.0 reduce-scatter.5.cloned.1.call-update
  203.6 0.6 copy-done.11
  204.3 0.6 dynamic-slice
  205.5 49.6 %all-reduce.9.cloned.1.call-done = bf16[4,10,128,128]{3,0,1,2:T(4,128)(2,1)} async-done(((bf16[4,10,128,128]{3,0,1,2:T(4,128)(2,1)}), bf16[4,10,128,128]{3,0,1,2:T(4,128)(2,1)}) %all-reduce.9.cloned.1.call-update) | async-done | bytes 1310736
  255.0 1.1 constant_dynamic-slice_fusion
  256.1 0.8 copy.82
  256.9 31.8 %reduce-scatter.3.cloned.1.call-done = bf16[4,10,32,128]{3,2,1,0:T(8,128)(2,1)} async-done(((bf16[4,10,128,128]{3,2,1,0:T(8,128)(2,1)}), bf16[4,10,32,128]{3,2,1,0:T(8,128)(2,1)}) %reduce-scatter.3.cloned.1.call-update) | async-done | bytes 327696 | tf_op jit(solution)/shard_map/reduce_scatter | solution.py:88
  288.7 32.9 %reduce-scatter.5.cloned.1.call-done = bf16[4,10,32,128]{3,2,1,0:T(8,128)(2,1)} async-done(((bf16[4,10,128,128]{3,2,1,0:T(8,128)(2,1)}), bf16[4,10,32,128]{3,2,1,0:T(8,128)(2,1)}) %reduce-scatter.5.cloned.1.call-update) | async-done | bytes 327696 | tf_op jit(solution)/shard_map/reduce_scatter | solution.py:91
  (19 shorter events, 0.0 us)
Async XLA Ops:
  8.0 63.6 %all-reduce.5.cloned.1.call-start = ((), (), s32[]{:S(2)}) async-start(), calls=%async_computation.2 | async-start | bytes 2097152 | tf_op jit(solution)/shard_map/psum | solution.py:9
  11.7 1.9 copy-start.7
  11.7 2.0 copy-start.8
  11.7 2.0 copy-start.4
  11.8 61.9 %all-gather.6.cloned.1.call-start = ((), (), s32[]{:S(2)}) async-start(), calls=%async_computation.4 | async-start | bytes 1638400 | tf_op jit(solution)/shard_map/all_gather | solution.py:35
  12.3 2.8 copy-start.9
  12.3 2.8 copy-start.10
  12.4 69.5 %all-gather.8.cloned.1.call-start = ((), (), s32[]{:S(2)}) async-start(), calls=%async_computation.5 | async-start | bytes 1638400 | tf_op jit(solution)/shard_map/all_gather | solution.py:36
  13.0 101.9 %all-gather.4.cloned.1.call-start = ((), (), s32[]{:S(2)}) async-start(), calls=%async_computation.3 | async-start | bytes 1638400 | tf_op jit(solution)/shard_map/all_gather | solution.py:37
  13.5 173.0 %all-reduce.7.cloned.1.call-start = ((), (), s32[]{:S(2)}) async-start(), calls=%async_computation.6 | async-start | bytes 2097152 | tf_op jit(solution)/shard_map/psum | solution.py:61
  73.6 8.3 %copy-start = (bf16[40,128,128]{2,1,0:T(8,128)(2,1)}, bf16[40,128,128]{2,1,0:T(8,128)(2,1)S(1)}, u32[]{:S(2)}) copy-start(bf16[40,128,128]{2,1,0:T(8,128)(2,1)S(1)} %gather_fusion) | copy-start | bytes 3932164
  83.9 31.0 %copy-start.5 = (f32[128,4,128]{0,2,1:T(8,128)}, f32[128,4,128]{0,2,1:T(8,128)S(1)}, u32[]{:S(2)}) copy-start(f32[128,4,128]{0,2,1:T(8,128)S(1)} %fusion.14) | copy-start | bytes 786436
  125.7 1.8 copy-start.2
  130.5 124.6 %all-reduce.9.cloned.1.call-start = ((), (), s32[]{:S(2)}) async-start(), calls=%async_computation.9 | async-start | bytes 2621440
  195.5 1.3 copy-start.1
  195.6 93.1 %reduce-scatter.3.cloned.1.call-start = ((), (), s32[]{:S(2)}) async-start(), calls=%async_computation.7 | async-start | bytes 1638400 | tf_op jit(solution)/shard_map/reduce_scatter | solution.py:88
  198.3 2.0 copy-start.3
  198.3 2.0 copy-start.6
  202.0 119.6 %reduce-scatter.5.cloned.1.call-start = ((), (), s32[]{:S(2)}) async-start(), calls=%async_computation.8 | async-start | bytes 1638400 | tf_op jit(solution)/shard_map/reduce_scatter | solution.py:91
  203.6 0.7 copy-start.11
Sparse Core Ops, SparseCore 0:
  12.0 59.5 all-reduce.4
  130.6 55.8 all-reduce.6
Sparse Core Ops, SparseCore 1:
  13.8 35.1 all-gather.5
  50.4 31.4 all-gather.7
  83.3 31.5 all-gather.3
  195.6 59.3 all-reduce.8
  257.9 30.7 reduce-scatter.2
  291.6 29.9 reduce-scatter.4
where the time goes:
time: 330 us; the launch traced here: 329 us
  waiting for transfers between devices  265 us (80%)
  local copies, waits for them, and re-layouts  22.4 us (7%)
  between operations  17.1 us (5%)
  matrix products  13.2 us (4%)
  other arithmetic  11.2 us (3%)
    psum x1, waiting for transfers between devices, broadcast(): return lax.psum(jnp.where(mine, shard, jnp.zeros_like(shard)), axis)  56.3 us
    psum x1, waiting for transfers between devices, shards(): lax.psum((partial_out - own_term).astype(jnp.bfloat16), 'dp')  56 us
    unnamed x9, waiting for transfers between devices  51.2 us
    reduce_scatter x1, waiting for transfers between devices, shards(): lax.psum_scatter(up_grad.astype(jnp.bfloat16), 'fsdp', scatter_dimension=...  32.9 us
    reduce_scatter x1, waiting for transfers between devices, shards(): lax.psum_scatter(gate_grad.astype(jnp.bfloat16), 'fsdp', scatter_dimensio...  31.8 us
    all_gather x1, waiting for transfers between devices, shards(): lax.all_gather(down_blocks, 'fsdp', axis=2, tiled=True)  30.9 us
    unnamed x29, local copies, waits for them, and re-layouts  7.28 us
  transfers between devices with their start and end apart: 8, of which 7 were waited for; matrix products, arithmetic and copies ran while one was open for 5% of the time, Pallas kernels for 0%

commit v1 on v0

--- a/solution.py
+++ b/solution.py
@@ -4,9 +4,15 @@
 from jax.sharding import PartitionSpec as P
 
 
+def gather_and_add(x, mesh_axis):
+    parts = lax.all_gather(x, mesh_axis, axis=0, tiled=False)
+    summed = parts.sum(axis=0)
+    return summed
+
+
 def broadcast(shard, axis, root):
     mine = lax.axis_index(axis) == root
-    return lax.psum(jnp.where(mine, shard, jnp.zeros_like(shard)), axis)
+    return gather_and_add(jnp.where(mine, shard, jnp.zeros_like(shard)), axis)
 
 
 def live_mask(counts, slot_count):

time: 330 us -> 383 us (1.16)
  waiting for transfers between devices: 265 us -> 314 us
  other arithmetic: 11.2 us -> 16.6 us
    psum x1 -> x0, waiting for transfers between devices: 56.3 us -> none  [broadcast(): return lax.psum(jnp.where(mine, shard, jnp.zeros_like(shard)), axis)]
    all_gather x0 -> x1, waiting for transfers between devices: none -> 52.8 us  [gather_and_add(): parts = lax.all_gather(x, mesh_axis, axis=0, tiled=False)]
    all_gather x1, waiting for transfers between devices: 0.03 us -> 27 us  [shards(): lax.all_gather(gate_blocks, 'fsdp', axis=2, tiled=True)]
    all_gather x1, waiting for transfers between devices: 5.83 us -> 31.3 us  [shards(): lax.all_gather(up_blocks, 'fsdp', axis=2, tiled=True)]
    reduce_sum x0 -> x1, other arithmetic: none -> 4.91 us  [gather_and_add(): summed = parts.sum(axis=0)]
  transfers between devices with their start and end apart: 8 -> 8, of which waited for: 7 -> 8; matrix products, arithmetic and copies ran while one was open for 5% -> 6% of each run, Pallas kernels for 0% -> 0%
where the time goes in v1:
time: 383 us; the launch traced here: 382 us
  waiting for transfers between devices  314 us (82%)
  local copies, waits for them, and re-layouts  22.4 us (6%)
  other arithmetic  16.6 us (4%)
  between operations  15.7 us (4%)
  matrix products  12.7 us (3%)
    psum x1, waiting for transfers between devices, shards(): lax.psum((partial_out - own_term).astype(jnp.bfloat16), 'dp')  55.9 us
    all_gather x1, waiting for transfers between devices, gather_and_add(): parts = lax.all_gather(x, mesh_axis, axis=0, tiled=False)  52.8 us
    unnamed x9, waiting for transfers between devices  51.6 us
    reduce_scatter x1, waiting for transfers between devices, shards(): lax.psum_scatter(up_grad.astype(jnp.bfloat16), 'fsdp', scatter_dimension=...  33 us
    reduce_scatter x1, waiting for transfers between devices, shards(): lax.psum_scatter(gate_grad.astype(jnp.bfloat16), 'fsdp', scatter_dimensio...  32 us
    all_gather x1, waiting for transfers between devices, shards(): lax.all_gather(up_blocks, 'fsdp', axis=2, tiled=True)  31.3 us
    all_gather x1, waiting for transfers between devices, shards(): lax.all_gather(down_blocks, 'fsdp', axis=2, tiled=True)  31 us
    all_gather x1, waiting for transfers between devices, shards(): lax.all_gather(gate_blocks, 'fsdp', axis=2, tiled=True)  27 us
  transfers between devices with their start and end apart: 8, of which 8 were waited for; matrix products, arithmetic and copies ran while one was open for 6% of the time, Pallas kernels for 0%

profile of v1, /device:TPU:0, one launch (start us, length us, event | category | flops | bytes accessed | tf_op | source)
XLA Modules:
  0.0 382.1 jit_solution(10308920849191856770)
XLA Ops:
  7.2 0.0 all-gather.5.cloned.1.call-start
  7.9 1.6 copy.83
  9.5 0.1 broadcast_select_fusion.3
  9.6 1.3 copy.84
  10.9 0.0 all-gather.5.cloned.1.call-update
  10.9 0.0 all-gather.9.cloned.1.call-start
  10.9 0.7 all-gather.9.cloned.1.call-update
  11.7 0.0 copy-start.9
  11.7 0.0 copy-start.10
  11.7 0.0 all-gather.11.cloned.1.call-start
  11.7 0.7 all-gather.11.cloned.1.call-update
  12.4 0.0 all-gather.7.cloned.1.call-start
  12.5 0.5 all-gather.7.cloned.1.call-update
  13.0 0.0 all-reduce.4.cloned.1.call-start
  13.1 0.1 reshape.104
  13.1 0.1 reshape.120
  13.2 1.3 copy.96
  14.6 0.6 iota_compare_fusion
  15.2 0.1 fusion.34
  15.2 52.8 %all-gather.5.cloned.1.call-done = bf16[8,128,4096]{2,1,0:T(8,128)(2,1)} async-done(((bf16[1,128,4096]{2,1,0:T(8,128)(2,1)}), bf16[8,128,4096]{2,1,0:T(8,128)(2,1)}) %all-gather.5.cloned.1.call-update) | async-done | bytes 8388624 | tf_op jit(solution)/shard_map/all_gather | solution.py:8
  68.0 4.9 %reduce_sum.12 = bf16[128,4096]{1,0:T(8,128)(2,1)S(1)} reduce(bf16[8,128,4096]{2,1,0:T(8,128)(2,1)} %all-gather.5.cloned.1.call-done, bf16[]{:T(256)} %constant.4.clone.1), dimensions={0}, to_apply=%region_0.1 | reduce | flops 3670016 | bytes 9437186 | tf_op jit(solution)/shard_map/reduce_sum | solution.py:9
  72.9 0.7 copy.85
  73.6 0.7 copy.86
  74.3 0.0 copy-start.11
  74.3 0.8 gather_fusion
  75.1 27.0 %all-gather.9.cloned.1.call-done = bf16[4,10,128,128]{3,2,1,0:T(8,128)(2,1)} async-done(((bf16[4,10,32,128]{3,2,1,0:T(8,128)(2,1)}), bf16[4,10,128,128]{3,2,1,0:T(8,128)(2,1)}) %all-gather.9.cloned.1.call-update) | async-done | bytes 1310736 | tf_op jit(solution)/shard_map/all_gather | solution.py:41
  102.2 2.0 fusion.11
  104.1 31.3 %all-gather.11.cloned.1.call-done = bf16[4,10,128,128]{3,2,1,0:T(8,128)(2,1)} async-done(((bf16[4,10,32,128]{3,2,1,0:T(8,128)(2,1)}), bf16[4,10,128,128]{3,2,1,0:T(8,128)(2,1)}) %all-gather.11.cloned.1.call-update) | async-done | bytes 1310736 | tf_op jit(solution)/shard_map/all_gather | solution.py:42
  135.4 2.0 fusion.14
  137.4 0.0 copy-start.5
  137.4 0.1 fusion.23
  137.5 31.0 %all-gather.7.cloned.1.call-done = bf16[4,10,128,128]{3,2,1,0:T(8,128)(2,1)} async-done(((bf16[4,10,32,128]{3,2,1,0:T(8,128)(2,1)}), bf16[4,10,128,128]{3,2,1,0:T(8,128)(2,1)}) %all-gather.7.cloned.1.call-update) | async-done | bytes 1310736 | tf_op jit(solution)/shard_map/all_gather | solution.py:43
  168.5 2.0 fusion.17
  170.5 2.1 copy.94
  172.6 0.2 broadcast_in_dim.49
  172.8 6.5 %scatter_fusion = f32[128,32,128]{2,0,1:T(8,128)S(1)} fusion(f32[128,32,128]{2,0,1:T(8,128)S(1)} %broadcast_in_dim.49, s32[40]{0:T(128)S(1)} %reshape.120, f32[40,128,128]{2,1,0:T(8,128)} %copy.94), kind=kCustom, calls=%fused_computation.2 | custom fusion | flops 655360 | bytes 7864480 | tf_op jit(solution)/shard_map/scatter-add | solution.py:64
  179.4 1.8 copy.95
  181.2 2.8 fusion
  184.0 0.0 all-reduce.4.cloned.1.call-update
  184.1 0.0 all-reduce.6.cloned.1.call-start
  184.1 55.9 %all-reduce.4.cloned.1.call-done = bf16[128,4096]{0,1:T(8,128)(2,1)} async-done(((bf16[128,4096]{0,1:T(8,128)(2,1)}), bf16[128,4096]{0,1:T(8,128)(2,1)}) %all-reduce.4.cloned.1.call-update) | async-done | bytes 1048592 | tf_op jit(solution)/shard_map/psum | solution.py:67
  240.0 1.4 multiply_convert_fusion.3
  241.5 0.7 copy.97
  242.1 0.8 gather_fusion.1
  242.9 0.8 copy.98
  243.7 1.6 fusion.1
  245.3 3.7 copy.103
  249.0 0.0 all-reduce.6.cloned.1.call-update
  249.0 0.0 reduce-scatter.3.cloned.1.call-start
  249.1 1.2 copy-done.1
  250.3 1.4 copy.87
  251.8 2.0 convolution_bitcast_fusion
  253.8 1.6 multiply_convert_fusion.2
  255.4 0.0 reduce-scatter.3.cloned.1.call-update
  255.4 0.0 reduce-scatter.5.cloned.1.call-start
  255.5 1.6 multiply_convert_fusion.1
  257.1 0.0 reduce-scatter.5.cloned.1.call-update
  257.1 0.6 copy-done.12
  257.7 0.6 dynamic-slice
  258.9 49.6 %all-reduce.6.cloned.1.call-done = bf16[4,10,128,128]{3,0,1,2:T(4,128)(2,1)} async-done(((bf16[4,10,128,128]{3,0,1,2:T(4,128)(2,1)}), bf16[4,10,128,128]{3,0,1,2:T(4,128)(2,1)}) %all-reduce.6.cloned.1.call-update) | async-done | bytes 1310736
  308.5 1.1 constant_dynamic-slice_fusion
  309.6 0.8 copy.104
  310.4 32.0 %reduce-scatter.3.cloned.1.call-done = bf16[4,10,32,128]{3,2,1,0:T(8,128)(2,1)} async-done(((bf16[4,10,128,128]{3,2,1,0:T(8,128)(2,1)}), bf16[4,10,32,128]{3,2,1,0:T(8,128)(2,1)}) %reduce-scatter.3.cloned.1.call-update) | async-done | bytes 327696 | tf_op jit(solution)/shard_map/reduce_scatter | solution.py:94
  342.3 33.0 %reduce-scatter.5.cloned.1.call-done = bf16[4,10,32,128]{3,2,1,0:T(8,128)(2,1)} async-done(((bf16[4,10,128,128]{3,2,1,0:T(8,128)(2,1)}), bf16[4,10,32,128]{3,2,1,0:T(8,128)(2,1)}) %reduce-scatter.5.cloned.1.call-update) | async-done | bytes 327696 | tf_op jit(solution)/shard_map/reduce_scatter | solution.py:97
  (24 shorter events, 0.1 us)
Async XLA Ops:
  7.2 60.9 %all-gather.5.cloned.1.call-start = ((), (), s32[]{:S(2)}) async-start(), calls=%async_computation.2 | async-start | bytes 9437184 | tf_op jit(solution)/shard_map/all_gather | solution.py:8
  10.9 2.2 copy-start.7
  10.9 2.3 copy-start.8
  10.9 2.4 copy-start.4
  10.9 91.3 %all-gather.9.cloned.1.call-start = ((), (), s32[]{:S(2)}) async-start(), calls=%async_computation.4 | async-start | bytes 1638400 | tf_op jit(solution)/shard_map/all_gather | solution.py:41
  11.7 2.9 copy-start.9
  11.7 3.5 copy-start.10
  11.7 123.7 %all-gather.11.cloned.1.call-start = ((), (), s32[]{:S(2)}) async-start(), calls=%async_computation.5 | async-start | bytes 1638400 | tf_op jit(solution)/shard_map/all_gather | solution.py:42
  12.4 156.1 %all-gather.7.cloned.1.call-start = ((), (), s32[]{:S(2)}) async-start(), calls=%async_computation.3 | async-start | bytes 1638400 | tf_op jit(solution)/shard_map/all_gather | solution.py:43
  13.0 227.0 %all-reduce.4.cloned.1.call-start = ((), (), s32[]{:S(2)}) async-start(), calls=%async_computation.6 | async-start | bytes 2097152 | tf_op jit(solution)/shard_map/psum | solution.py:67
  74.3 27.9 %copy-start.11 = (pred[4,10]{1,0:T(4,128)(4,1)S(1)}, pred[4,10]{1,0:T(4,128)(4,1)}, u32[]{:S(2)}) copy-start(pred[4,10]{1,0:T(4,128)(4,1)} %get-tuple-element.20) | copy-start | bytes 124
  75.1 60.3 %copy-start = (bf16[40,128,128]{2,1,0:T(8,128)(2,1)}, bf16[40,128,128]{2,1,0:T(8,128)(2,1)S(1)}, u32[]{:S(2)}) copy-start(bf16[40,128,128]{2,1,0:T(8,128)(2,1)S(1)} %gather_fusion) | copy-start | bytes 3932164
  137.4 31.1 %copy-start.5 = (f32[128,4,128]{0,2,1:T(8,128)}, f32[128,4,128]{0,2,1:T(8,128)S(1)}, u32[]{:S(2)}) copy-start(f32[128,4,128]{0,2,1:T(8,128)S(1)} %fusion.14) | copy-start | bytes 786436
  179.3 1.8 copy-start.2
  184.1 124.5 %all-reduce.6.cloned.1.call-start = ((), (), s32[]{:S(2)}) async-start(), calls=%async_computation.9 | async-start | bytes 2621440
  249.0 1.3 copy-start.1
  249.0 93.3 %reduce-scatter.3.cloned.1.call-start = ((), (), s32[]{:S(2)}) async-start(), calls=%async_computation.7 | async-start | bytes 1638400 | tf_op jit(solution)/shard_map/reduce_scatter | solution.py:94
  251.8 2.0 copy-start.3
  251.8 2.0 copy-start.6
  255.4 119.9 %reduce-scatter.5.cloned.1.call-start = ((), (), s32[]{:S(2)}) async-start(), calls=%async_computation.8 | async-start | bytes 1638400 | tf_op jit(solution)/shard_map/reduce_scatter | solution.py:97
  257.0 0.7 copy-start.12
Sparse Core Ops, SparseCore 0:
  11.0 56.9 all-gather.4
  69.6 32.5 all-gather.8
  103.7 31.6 all-gather.10
  136.8 31.6 all-gather.6
  184.2 55.8 all-reduce.3
  249.2 59.3 all-reduce.5
  311.4 30.9 reduce-scatter.2
  345.2 30.0 reduce-scatter.4
